TPU v7x, 128 devices: a whole 4x4x4 slice. The times are simulated.
128 devices in a mesh: row: 8 (over x, y_lo), col: 16 (over z, y_hi, core).
Axes of the slice: x: 4, y: 4 (y_hi: 2, y_lo: 2; y = y_hi * 2 + y_lo), z: 4, core: 2. Of those that a mesh axis runs over, the one named last changes fastest.
Arguments:
- alignment_left: bfloat16 [1024, 16384], P(('row', 'col')), may hold values from -6 to 6
- alignment_right: bfloat16 [512, 32768], P('row', 'col'), may hold values from -6 to 6
- pair_features: bfloat16 [1024, 1024, 128], P('row', 'col'), may hold values from -6 to 6
- output_weight: bfloat16 [1024, 128], replicated, may hold values from -4 to 4
- output_bias: float32 [128], replicated, may hold values from -4 to 4
- norm_scale_gain: float32 [128], replicated, may hold values from 0.1 to 1.9
- projection_weight: bfloat16 [128, 512], replicated, may hold values from -0.5 to 0.5
- gate_offset_bias: float32 [128], replicated, may hold values from -4 to 4
Outputs:
- new_pair: bfloat16 [1024, 1024, 128], P('row', 'col')
- projections: bfloat16 [1024, 512, 1024], P('row', 'col')
All inputs are finite; a program needn't handle non-finite values.
Results may differ from a plain program's by a relative error of at most 0.0058.
Values may be sent and summed in bfloat16 or wider, within the bound.
A program may use at most 192 MiB of HBM per device.

v0:
```python
import jax
import jax.numpy as jnp
from jax import lax
from jax.sharding import PartitionSpec as P

CHANNEL_WIDTH = 32


norm_eps = 1e-05


def project(values, norm_scale_gain, projection_weight, gate_offset_bias):
    widened = values.astype(jnp.float32)
    average = jnp.mean(widened, axis=-1, keepdims=True)
    centred = widened - average
    variance = jnp.mean(centred * centred, axis=-1, keepdims=True)
    normed = (centred * lax.rsqrt(variance + norm_eps) * norm_scale_gain).astype(jnp.bfloat16)
    projected = jnp.dot(normed, projection_weight, preferred_element_type=jnp.float32)
    quarter = projection_weight.shape[1] // 4
    head_part = projected[..., : 3 * quarter]
    gate_part = jax.nn.sigmoid(projected[..., 3 * quarter :] + gate_offset_bias)
    return jnp.concatenate([head_part, gate_part], axis=-1).astype(jnp.bfloat16)


def shards(
    alignment_left,
    alignment_right,
    pair_features,
    output_weight,
    output_bias,
    norm_scale_gain,
    projection_weight,
    gate_offset_bias,
):
    col_count = lax.axis_size("col")
    tile_rows, tile_cols, channels = pair_features.shape
    right_complete = lax.all_gather(alignment_right, "row", axis=0, tiled=True)
    alignment_depth = right_complete.shape[0]
    alignment_portion = lax.all_gather(alignment_left, "col", axis=0, tiled=True)
    residue_total = alignment_portion.shape[0]
    shaped = alignment_portion.reshape(residue_total, CHANNEL_WIDTH, alignment_depth)
    channel_products = lax.dot_general(
        shaped, right_complete, (((2,), (0,)), ((), ())), preferred_element_type=jnp.float32
    )
    outer_product_average = (channel_products / alignment_depth).astype(jnp.bfloat16)
    outer_product_average = outer_product_average.reshape(
        residue_total, CHANNEL_WIDTH, tile_cols, CHANNEL_WIDTH
    ).transpose(0, 2, 1, 3)
    outer_product_average = outer_product_average.reshape(
        residue_total * tile_cols, CHANNEL_WIDTH * CHANNEL_WIDTH
    )
    update = (
        jnp.dot(outer_product_average, output_weight, preferred_element_type=jnp.float32)
        + output_bias
    )
    fresh = pair_features.astype(jnp.float32).reshape(residue_total * tile_cols, channels) + update
    new_pair = fresh.astype(jnp.bfloat16).reshape(residue_total, tile_cols, channels)
    group_width = projection_weight.shape[1] // col_count
    residues = tile_cols * col_count
    projected = project(new_pair, norm_scale_gain, projection_weight, gate_offset_bias)
    across = lax.all_to_all(
        projected.reshape(tile_rows, tile_cols, col_count, group_width),
        "col",
        split_axis=2,
        concat_axis=1,
        tiled=True,
    )
    down_moved = lax.all_to_all(
        across.reshape(tile_rows, residues, group_width),
        "row",
        split_axis=1,
        concat_axis=0,
        tiled=True,
    )
    result = down_moved.transpose(1, 2, 0)
    return (new_pair, result)


def solution(mesh):
    placed = (
        P(("row", "col"), None),
        P("row", "col"),
        P("row", "col", None),
        P(),
        P(),
        P(),
        P(),
        P(),
    )
    return jax.shard_map(
        shards,
        mesh=mesh,
        in_specs=placed,
        out_specs=(P("row", "col", None), P("row", "col", None)),
        check_vma=False,
    )
```

profile of v0, /device:TPU:1, one launch (start us, length us, event | category | flops | bytes accessed | tf_op | source)
XLA Modules:
  0.0 531.3 jit_solution(17028867448497850056)
XLA Ops:
  7.2 0.0 copy-start
  7.2 0.0 all-gather.3.cloned.1.call-start
  7.2 0.7 all-gather.3.cloned.1.call-update
  7.9 0.0 all-gather.5.cloned.1.call-start
  8.0 0.7 all-gather.5.cloned.1.call-update
  8.7 60.5 %all-gather.3.cloned.1.call-done = bf16[128,16384]{1,0:T(8,128)(2,1)} async-done(((bf16[8,16384]{1,0:T(8,128)(2,1)}), bf16[128,16384]{1,0:T(8,128)(2,1)}) %all-gather.3.cloned.1.call-update) | async-done | bytes 4194320 | tf_op jit(solution)/shard_map/all_gather | solution.py:39
  69.1 6.4 %copy.27 = bf16[128,16384]{0,1:T(8,128)(2,1)} copy(bf16[128,16384]{1,0:T(8,128)(2,1)} %all-gather.3.cloned.1.call-done) | data formatting | bytes 8388608 | tf_op jit(solution)/shard_map/all_gather | solution.py:39
  75.5 42.3 %all-gather.5.cloned.1.call-done = bf16[512,2048]{1,0:T(8,128)(2,1)} async-done(((bf16[64,2048]{1,0:T(8,128)(2,1)}), bf16[512,2048]{1,0:T(8,128)(2,1)}) %all-gather.5.cloned.1.call-update) | async-done | bytes 2097168 | tf_op jit(solution)/shard_map/all_gather | solution.py:37
  117.8 14.9 %multiply_convert_fusion = bf16[128,32,2048]{2,0,1:T(8,128)(2,1)} fusion(bf16[128,32,512]{0,2,1:T(8,128)(2,1)} %bitcast.39, bf16[512,2048]{1,0:T(8,128)(2,1)} %all-gather.5.cloned.1.call-done), kind=kOutput, calls=%fused_computation | convolution fusion | flops 8606711808 | bytes 23068672 | tf_op jit(solution)/shard_map/dot_general | solution.py:42
  132.7 22.5 %copy.29 = bf16[128,32,2048]{0,2,1:T(8,128)(2,1)} copy(bf16[128,32,2048]{2,0,1:T(8,128)(2,1)} %multiply_convert_fusion) | data formatting | bytes 33554432 | tf_op jit(solution)/shard_map/convert_element_type | solution.py:45
  155.2 34.1 %copy.30 = bf16[128,64,32,32]{1,0,3,2:T(8,128)(2,1)} copy(bf16[128,64,32,32]{0,3,1,2:T(8,128)(2,1)} %bitcast.32) | data formatting | bytes 33554432 | tf_op jit(solution)/shard_map/transpose | solution.py:48
  189.3 0.0 copy-start.6
  189.3 44.0 %reshape.65 = bf16[8192,1024]{0,1:T(8,128)(2,1)} reshape(bf16[128,64,32,32]{1,0,3,2:T(8,128)(2,1)} %copy.30) | data formatting | bytes 33554432 | tf_op jit(solution)/shard_map/reshape | solution.py:49
  233.4 0.0 copy-done
  233.4 0.0 copy-done.6
  233.4 0.0 copy-start.4
  233.4 11.9 %convert_reduce_fusion = (f32[8192]{0:T(1024)S(1)}, bf16[8192,128]{1,0:T(8,128)(2,1)S(1)}) fusion(f32[128]{0:T(128)S(1)} %copy-done.6, bf16[8192,1024]{0,1:T(8,128)(2,1)} %reshape.65, bf16[1024,128]{1,0:T(8,128)(2,1)S(1)} %copy-done, bf16[8192,128]{1,0:T(8,128)(2,1)} %bitcast.40), kind=kOutput, calls=%fused_computation.7 | convolution fusion | flops 2153766912 | bytes 21266944 | tf_op jit(solution)/shard_map/dot_general | solution.py:53
  245.3 0.0 copy-start.2
  245.3 0.0 copy-start.3
  245.3 0.1 div.20
  245.4 2.3 fusion.3
  247.8 0.1 rsqrt.12
  247.9 0.0 copy-done.4
  247.9 3.8 multiply_convert_fusion.1
  251.7 0.0 copy-done.2
  251.7 0.0 copy-done.3
  251.7 8.1 %fusion.10 = f32[128,64,512]{2,0,1:T(8,128)} fusion(bf16[128,64,128]{2,1,0:T(8,128)(2,1)S(1)} %multiply_convert_fusion.1, bf16[128,512]{1,0:T(8,128)(2,1)S(1)} %copy-done.3), kind=kOutput, calls=%fused_computation.18 | convolution fusion | flops 1073741824 | bytes 19005440 | tf_op jit(solution)/shard_map/dot_general | solution.py:18
  259.8 0.0 copy-start.5
  259.8 5.6 %slice.23 = bf16[128,64,384]{2,0,1:T(8,128)(2,1)S(1)} slice(f32[128,64,512]{2,0,1:T(8,128)} %fusion.10), slice={[0:128], [0:64], [0:384]} | slice | bytes 12582912 | tf_op jit(solution)/shard_map/slice | solution.py:20
  265.5 0.0 copy-done.5
  265.5 4.6 fusion.8
  270.1 6.2 %pad_maximum_fusion = bf16[128,64,512]{2,0,1:T(8,128)(2,1)} fusion(bf16[128,64,128]{2,0,1:T(8,128)(2,1)} %fusion.8, bf16[128,64,384]{2,0,1:T(8,128)(2,1)S(1)} %slice.23), kind=kLoop, calls=%fused_computation.5 | loop fusion | flops 16777216 | bytes 16777216 | tf_op jit(solution)/shard_map/concatenate | solution.py:22
  276.3 12.0 %copy.32 = bf16[128,64,512]{0,2,1:T(8,128)(2,1)} copy(bf16[128,64,512]{2,0,1:T(8,128)(2,1)} %pad_maximum_fusion) | data formatting | bytes 16777216 | tf_op jit(solution)/shard_map/concatenate | solution.py:22
  288.3 9.0 %copy.33 = bf16[128,64,16,32]{0,3,1,2:T(8,128)(2,1)} copy(bf16[128,64,16,32]{0,3,2,1:T(8,128)(2,1)} %bitcast.33) | data formatting | bytes 16777216 | tf_op jit(solution)/shard_map/convert_element_type | solution.py:22
  297.3 104.0 %all_to_all.33 = bf16[128,64,16,32]{0,3,1,2:T(8,128)(2,1)S(1)} all-to-all(bf16[128,64,16,32]{0,3,1,2:T(8,128)(2,1)} %copy.33), channel_id=1, replica_groups=mesh['row'=8,'col'=16] {'col'}, dimensions={2} | all-to-all | bytes 16777216 | tf_op jit(solution)/shard_map/all_to_all | solution.py:61
  401.2 96.3 %all_to_all.34 = bf16[128,1024,32]{0,2,1:T(8,128)(2,1)} all-to-all(bf16[128,1024,32]{0,2,1:T(8,128)(2,1)S(1)} %bitcast.34), channel_id=1, replica_groups=mesh['row'=8,'col'=16] {'row'}, dimensions={1} | all-to-all | bytes 16777216 | tf_op jit(solution)/shard_map/all_to_all | solution.py:68
  497.5 13.3 %copy.34 = bf16[8,128,128,32]{2,3,1,0:T(8,128)(2,1)} copy(bf16[8,128,128,32]{1,3,2,0:T(8,128)(2,1)} %bitcast.35) | data formatting | bytes 16777216 | tf_op jit(solution)/shard_map/all_to_all | solution.py:68
  510.8 0.0 copy-start.1
  510.8 13.6 %copy.35 = bf16[128,32,1024]{2,1,0:T(8,128)(2,1)} copy(bf16[128,32,1024]{0,1,2:T(8,128)(2,1)} %bitcast.36) | data formatting | bytes 16777216
  524.4 0.0 copy-done.1
  (2 shorter events, 0.0 us)
Async XLA Ops:
  7.2 226.2 %copy-start = (bf16[1024,128]{1,0:T(8,128)(2,1)S(1)}, bf16[1024,128]{1,0:T(8,128)(2,1)}, u32[]{:S(2)}) copy-start(bf16[1024,128]{1,0:T(8,128)(2,1)} %param.11) | copy-start | bytes 786436
  7.2 62.0 %all-gather.3.cloned.1.call-start = ((), (), s32[]{:S(2)}) async-start(), calls=%async_computation.2 | async-start | bytes 4456448 | tf_op jit(solution)/shard_map/all_gather | solution.py:39
  7.9 109.9 %all-gather.5.cloned.1.call-start = ((), (), s32[]{:S(2)}) async-start(), calls=%async_computation.3 | async-start | bytes 2359296 | tf_op jit(solution)/shard_map/all_gather | solution.py:37
  189.3 44.0 %copy-start.6 = (f32[128]{0:T(128)S(1)}, f32[128]{0:T(128)}, u32[]{:S(2)}) copy-start(f32[128]{0:T(128)} %param.12) | copy-start | bytes 1540
  233.4 14.5 %copy-start.4 = (f32[128]{0:T(128)S(1)}, f32[128]{0:T(128)}, u32[]{:S(2)}) copy-start(f32[128]{0:T(128)} %param.13) | copy-start | bytes 1540
  245.3 6.4 %copy-start.2 = (bf16[8192,128]{1,0:T(8,128)(2,1)}, bf16[8192,128]{1,0:T(8,128)(2,1)S(1)}, u32[]{:S(2)}) copy-start(bf16[8192,128]{1,0:T(8,128)(2,1)S(1)} %get-tuple-element.7) | copy-start | bytes 6291460
  245.3 6.4 %copy-start.3 = (bf16[128,512]{1,0:T(8,128)(2,1)S(1)}, bf16[128,512]{1,0:T(8,128)(2,1)}, u32[]{:S(2)}) copy-start(bf16[128,512]{1,0:T(8,128)(2,1)} %param.14) | copy-start | bytes 393220
  259.8 5.6 %copy-start.5 = (f32[128]{0:T(128)S(1)}, f32[128]{0:T(128)}, u32[]{:S(2)}) copy-start(f32[128]{0:T(128)} %param.15) | copy-start | bytes 1540
  510.8 13.6 %copy-start.1 = (bf16[1024,128]{1,0:T(8,128)(2,1)S(1)}, bf16[1024,128]{1,0:T(8,128)(2,1)}, u32[]{:S(2)}) copy-start(bf16[1024,128]{1,0:T(8,128)(2,1)} %param.11) | copy-start | bytes 786436
Sparse Core Ops, SparseCore 0:
  10.5 58.6 all-gather.2
  70.8 46.9 all-gather.4
where the time goes:
time: 536 us; the launch traced here: 531 us
  blocking collectives  200 us (37%)
  local copies, waits for them, and re-layouts  161 us (30%)
  waiting for transfers between devices  104 us (19%)
  matrix products  35 us (7%)
  other arithmetic  16.9 us (3%)
  between operations  14.1 us (3%)
    all_to_all x1, blocking collectives, shards(): lax.all_to_all(projected.reshape(tile_rows, tile_cols, col_count, group_w...  104 us
    all_to_all x1, blocking collectives, shards(): lax.all_to_all(across.reshape(tile_rows, residues, group_width), 'row', s...  96.3 us
    all_gather x1, waiting for transfers between devices, shards(): lax.all_gather(alignment_left, 'col', axis=0, tiled=True)  60.5 us
    reshape x1, local copies, waits for them, and re-layouts, shards(): outer_product_average.reshape(residue_total * tile_cols, CHANNEL_WIDTH *...  44 us
    all_gather x1, waiting for transfers between devices, shards(): right_complete = lax.all_gather(alignment_right, 'row', axis=0, tiled=True)  42.3 us
    transpose x1, local copies, waits for them, and re-layouts, shards(): outer_product_average = outer_product_average.reshape(residue_total, CHAN...  34.1 us
    convert_element_type x1, local copies, waits for them, and re-layouts, shards(): (channel_products / alignment_depth).astype(jnp.bfloat16)  22.5 us
    dot_general x1, matrix products, shards(): lax.dot_general(shaped, right_complete, (((2,), (0,)), ((), ())), preferr...  14.9 us
  transfers between devices with their start and end apart: 2, of which 2 were waited for; matrix products, arithmetic and copies ran while one was open for 1% of the time, Pallas kernels for 0%

commit v1 on v0

v1 whole, which is shorter than its diff:
```python
import functools

import jax
import jax.numpy as jnp
from jax import lax
from jax.experimental import pallas as pl
from jax.experimental.pallas import tpu as pltpu
from jax.sharding import PartitionSpec as P

MESH = pl.DeviceIdType.MESH
bf16, f32 = jnp.bfloat16, jnp.float32
norm_eps = 1e-05

ROWS, COLS = 8, 16
TI, TJ, C, PROJ = 128, 64, 128, 512
W, S = 32, 512
GROUP = PROJ // COLS
JN = 4
NT = TJ // JN
LAG = 2


def kernel(
    left_hbm, right_hbm, pair_ref, weight_ref, bias_ref, gain_ref, proj_ref, gate_ref,
    new_ref, out,
    left, right, block_weight, proj_t, gate_t, outer, pair_f, new_f, send_buf, stage,
    load_sem, send1, recv1, send2, recv2,
):
    row, col = lax.axis_index("row"), lax.axis_index("col")
    y_lo = row % 2
    x2 = row - y_lo
    y_hi = (col // 2) % 2

    for c1 in range(W):
        pltpu.make_async_copy(left_hbm.at[:, pl.ds(c1 * S, S)], left.at[c1], load_sem.at[0]).start()
    for u in range(8):
        pltpu.make_async_copy(right_hbm.at[:, pl.ds(u * 256, 256)], right.at[u], load_sem.at[1]).start()

    block_weight[...] = jnp.zeros_like(block_weight)

    def fill(c1, _):
        w = weight_ref[pl.ds(pl.multiple_of(c1 * W, W), W), :]
        for j in range(4):
            block_weight[pl.ds(pl.multiple_of(c1 * 128 + j * W, W), W), j * C : (j + 1) * C] = w
        return 0

    lax.fori_loop(0, W, fill, 0)
    proj_t[...] = proj_ref[...].astype(f32).T.astype(bf16)
    gate_t[...] = jnp.broadcast_to(gate_ref[...], (C, C)).T

    pltpu.make_async_copy(left, left, load_sem.at[0]).wait()
    pltpu.make_async_copy(right, right, load_sem.at[1]).wait()

    def target(core, t, r):
        j0 = pl.multiple_of(core * TJ + t * JN, JN)
        return out.at[pl.ds(j0, JN), :, pl.ds(pl.multiple_of(r * TI, TI), TI)]

    def send(t):
        pltpu.make_async_copy(send_buf.at[t, col], stage.at[t, col], recv1.at[t, col]).start()

        def body(k, _):
            c2 = lax.bitwise_xor(col, k)
            r2 = x2 + (y_lo + y_hi + (c2 // 2) % 2) % 2
            pltpu.make_async_remote_copy(
                src_ref=send_buf.at[t, c2], dst_ref=stage.at[t, col], send_sem=send1, recv_sem=recv1.at[t, col],
                device_id=(r2, c2), device_id_type=MESH,
            ).start()
            return 0

        lax.fori_loop(1, COLS, body, 0)

    def forward(t):
        def piece(q, core, local):
            r2 = lax.bitwise_xor(row, q)
            origin = r2 * 2 + core
            r_origin = x2 + (y_lo + r2 % 2 + y_hi) % 2
            here = stage.at[t, origin]
            pltpu.make_async_copy(here, here, recv1.at[t, origin]).wait()
            if local:
                pltpu.make_async_copy(here, target(core, t, r_origin), recv2).start()
            else:
                pltpu.make_async_remote_copy(
                    src_ref=here, dst_ref=target(core, t, r_origin), send_sem=send2, recv_sem=recv2,
                    device_id=(r2, col), device_id_type=MESH,
                ).start()

        piece(0, 0, True)
        piece(0, 1, True)

        def body(m, _):
            piece(m // 2, m % 2, False)
            return 0

        lax.fori_loop(2, COLS, body, 0)

    def sixteen(v, _):
        j16 = pl.multiple_of(v * 16, 16)
        pair_f[...] = pair_ref[:, pl.ds(j16, 16), :].astype(f32).reshape(TI * 16, C)
        for half in range(2):
            u = v * 2 + half

            def products(b, _):
                lhs = left[pl.ds(b * 4, 4)].reshape(4 * TI, S)
                p = jnp.dot(lhs, right[u], preferred_element_type=f32)
                p = (p * (1.0 / S)).astype(bf16)
                for k in range(4):
                    for g in range(2):
                        outer[g * TI : (g + 1) * TI, pl.ds(pl.multiple_of(b * 512 + k * 128, 128), 128)] = p[
                            k * TI : (k + 1) * TI, g * 128 : (g + 1) * 128
                        ]
                return 0

            lax.fori_loop(0, W // 4, products, 0)
            update = jnp.dot(outer[...], block_weight[...], preferred_element_type=f32)
            for g in range(2):
                t = v * 4 + half * 2 + g
                for pairs in range(2):
                    both = []
                    for jj in range(2):
                        j = pairs * 2 + jj
                        j_in = half * 8 + g * 4 + j
                        add = update[g * TI : (g + 1) * TI, j * C : (j + 1) * C] + bias_ref[...]
                        fresh = (pair_f[pl.ds(j_in, TI, stride=16), :] + add).astype(bf16).astype(f32)
                        new_f[pl.ds(j_in, TI, stride=16), :] = fresh
                        average = jnp.mean(fresh, axis=-1, keepdims=True)
                        centred = fresh - average
                        variance = jnp.mean(centred * centred, axis=-1, keepdims=True)
                        both.append((centred * lax.rsqrt(variance + norm_eps) * gain_ref[...]).astype(bf16))
                    normed = jnp.concatenate(both, axis=0)
                    raw = lax.dot_general(
                        proj_t[...], normed, (((1,), (1,)), ((), ())), preferred_element_type=f32
                    )
                    for jj in range(2):
                        mine = raw[:, jj * TI : (jj + 1) * TI]
                        gate = jax.nn.sigmoid(mine[384:] + gate_t[...])
                        send_buf[t, 0:12, pairs * 2 + jj] = mine[:384].astype(bf16).reshape(12, GROUP, TI)
                        send_buf[t, 12:16, pairs * 2 + jj] = gate.astype(bf16).reshape(4, GROUP, TI)
                send(t)

                @pl.when(t >= LAG)
                def _():
                    forward(t - LAG)

        new_ref[:, pl.ds(j16, 16), :] = new_f[...].astype(bf16).reshape(TI, 16, C)
        return 0

    lax.fori_loop(0, TJ // 16, sixteen, 0)
    for t in range(NT - LAG, NT):
        forward(t)
    sent = send_buf.at[:, pl.ds(0, COLS - 1)]
    pltpu.make_async_copy(sent, sent, send1).wait()
    sent = stage.at[:, pl.ds(0, COLS - 2)]
    pltpu.make_async_copy(sent, sent, send2).wait()
    pltpu.make_async_copy(stage, stage, recv2).wait()


def shards(
    alignment_left, alignment_right, pair_features, output_weight, output_bias, norm_scale_gain, projection_weight,
    gate_offset_bias,
):
    right = lax.all_gather(alignment_right, "row", axis=0, tiled=True)
    left = lax.all_gather(alignment_left, "col", axis=0, tiled=True)
    vmem, anywhere = pl.BlockSpec(memory_space=pltpu.VMEM), pl.BlockSpec(memory_space=pl.ANY)
    return pl.pallas_call(
        kernel,
        out_shape=(
            jax.ShapeDtypeStruct((TI, TJ, C), bf16),
            jax.ShapeDtypeStruct((2 * TJ, GROUP, ROWS * TI), bf16),
        ),
        in_specs=[anywhere, anywhere] + [vmem] * 6,
        out_specs=(vmem, anywhere),
        scratch_shapes=[
            pltpu.VMEM((W, TI, S), bf16),
            pltpu.VMEM((8, S, 256), bf16),
            pltpu.VMEM((4 * W * W, 4 * C), bf16),
            pltpu.VMEM((PROJ, C), bf16),
            pltpu.VMEM((C, C), f32),
            pltpu.VMEM((2 * TI, W * 128), bf16),
            pltpu.VMEM((TI * 16, C), f32),
            pltpu.VMEM((TI * 16, C), f32),
            pltpu.VMEM((NT, COLS, JN, GROUP, TI), bf16),
            pltpu.VMEM((NT, COLS, JN, GROUP, TI), bf16),
            pltpu.SemaphoreType.DMA((2,)),
            pltpu.SemaphoreType.DMA,
            pltpu.SemaphoreType.DMA((NT, COLS)),
            pltpu.SemaphoreType.DMA,
            pltpu.SemaphoreType.DMA,
        ],
        compiler_params=pltpu.CompilerParams(has_side_effects=True, vmem_limit_bytes=62 << 20),
        name="pair_update",
    )(
        left, right, pair_features, output_weight, output_bias.reshape(1, C), norm_scale_gain.reshape(1, C),
        projection_weight, gate_offset_bias.reshape(1, C),
    )


def solution(mesh):
    placed = (P(("row", "col"), None), P("row", "col"), P("row", "col", None), P(), P(), P(), P(), P())
    return jax.shard_map(
        shards,
        mesh=mesh,
        in_specs=placed,
        out_specs=(P("row", "col", None), P("row", "col", None)),
        check_vma=False,
    )
```

time: 536 us -> 268 us (0.50)
  blocking collectives: 200 us -> 0 us
  local copies, waits for them, and re-layouts: 161 us -> 11.7 us
  Pallas kernels: 0 us -> 126 us
  matrix products: 35 us -> 0 us
  other arithmetic: 16.9 us -> 0 us
  waiting for transfers between devices: 104 us -> 115 us
    all_to_all x2 -> x0, blocking collectives: 200 us -> none  [the longest x1 104 us: shards(): lax.all_to_all(projected.reshape(tile_rows, tile_cols, col_count, group_w...]
    pallas_call x0 -> x1, Pallas kernels: none -> 126 us  [shards(): pl.pallas_call(kernel, out_shape=(jax.ShapeDtypeStruct((TI, TJ, C), bf16)...]
    reshape x1 -> x0, local copies, waits for them, and re-layouts: 44 us -> none  [shards(): outer_product_average.reshape(residue_total * tile_cols, CHANNEL_WIDTH *...]
    dot_general x3 -> x0, matrix products: 35 us -> none  [the longest x1 14.9 us: shards(): lax.dot_general(shaped, right_complete, (((2,), (0,)), ((), ())), preferr...]
    transpose x1 -> x0, local copies, waits for them, and re-layouts: 34.1 us -> none  [shards(): outer_product_average = outer_product_average.reshape(residue_total, CHAN...]
    convert_element_type x2 -> x0, local copies, waits for them, and re-layouts: 31.5 us -> none  [the longest x1 22.5 us: shards(): (channel_products / alignment_depth).astype(jnp.bfloat16)]
    all_to_all x1 -> x0, local copies, waits for them, and re-layouts: 13.3 us -> none  [shards(): lax.all_to_all(across.reshape(tile_rows, residues, group_width), 'row', s...]
    concatenate x1 -> x0, local copies, waits for them, and re-layouts: 12 us -> none  [project(): return jnp.concatenate([head_part, gate_part], axis=-1).astype(jnp.bfloat16)]
  transfers between devices with their start and end apart: 2 -> 2, of which waited for: 2 -> 2; matrix products, arithmetic and copies ran while one was open for 1% -> 0% of each run, Pallas kernels for 0% -> 0%
where the time goes in v1:
time: 268 us; the launch traced here: 267 us
  Pallas kernels  126 us (47%)
  waiting for transfers between devices  115 us (43%)
  between operations  14 us (5%)
  local copies, waits for them, and re-layouts  11.7 us (4%)
    pallas_call x1, Pallas kernels, shards(): pl.pallas_call(kernel, out_shape=(jax.ShapeDtypeStruct((TI, TJ, C), bf16)...  126 us
    all_gather x1, waiting for transfers between devices, shards(): left = lax.all_gather(alignment_left, 'col', axis=0, tiled=True)  60.1 us
    all_gather x1, waiting for transfers between devices, shards(): right = lax.all_gather(alignment_right, 'row', axis=0, tiled=True)  53.9 us
    unnamed x2, local copies, waits for them, and re-layouts  11.7 us
  transfers between devices with their start and end apart: 2, of which 2 were waited for; matrix products, arithmetic and copies ran while one was open for 0% of the time, Pallas kernels for 0%

profile of v1, /device:TPU:1, one launch (start us, length us, event | category | flops | bytes accessed | tf_op | source)
XLA Modules:
  0.0 267.3 jit_solution(8521727978542964795)
XLA Ops:
  7.2 0.0 all-gather.5.cloned.1.call-start
  7.2 0.7 all-gather.5.cloned.1.call-update
  7.9 0.0 all-gather.3.cloned.1.call-start
  7.9 0.7 all-gather.3.cloned.1.call-update
  8.6 53.9 %all-gather.5.cloned.1.call-done.right_hbm = bf16[512,2048]{1,0:T(8,128)(2,1)} async-done(((bf16[64,2048]{1,0:T(8,128)(2,1)}), bf16[512,2048]{1,0:T(8,128)(2,1)}) %all-gather.5.cloned.1.call-update) | async-done | bytes 2097168 | tf_op jit(solution)/shard_map/all_gather | solution.py:161
  62.5 60.1 %all-gather.3.cloned.1.call-done.left_hbm = bf16[128,16384]{1,0:T(8,128)(2,1)} async-done(((bf16[8,16384]{1,0:T(8,128)(2,1)}), bf16[128,16384]{1,0:T(8,128)(2,1)}) %all-gather.3.cloned.1.call-update) | async-done | bytes 4194320 | tf_op jit(solution)/shard_map/all_gather | solution.py:162
  122.6 126.1 %pair_update.1 = (bf16[128,64,128]{2,1,0:T(8,128)(2,1)}, bf16[128,32,1024]{2,1,0:T(8,128)(2,1)}) custom-call(bf16[128,16384]{1,0:T(8,128)(2,1)} %all-gather.3.cloned.1.call-done.left_hbm, bf16[512,2048]{1,0:T(8,128)(2,1)} %all-gather.5.cloned.1.call-done.right_hbm, bf16[128,64,128]{2,1,0:T(8,128)(2,1)} %pair_ref.1, bf16[1024,128]{1,0:T(8,128)(2,1)} %weight_ref.1, ...), custom_call_target="tpu_custom_call" | custom-call | tf_op jit(solution)/shard_map/pair_update/pallas_call | solution.py:164
  248.8 3.1 %copy.12 = bf16[128,64,128]{2,1,0:T(8,128)(2,1)} copy(bf16[128,64,128]{2,1,0:T(8,128)(2,1)} %get-tuple-element.4) | data formatting | bytes 4194304
  251.8 8.6 %copy.13 = bf16[128,32,1024]{2,1,0:T(8,128)(2,1)} copy(bf16[128,32,1024]{2,1,0:T(8,128)(2,1)} %get-tuple-element.5) | data formatting | bytes 16777216
Async XLA Ops:
  7.2 55.4 %all-gather.5.cloned.1.call-start = ((), (), s32[]{:S(2)}) async-start(), calls=%async_computation.1 | async-start | bytes 2359296 | tf_op jit(solution)/shard_map/all_gather | solution.py:161
  7.9 114.7 %all-gather.3.cloned.1.call-start = ((), (), s32[]{:S(2)}) async-start(), calls=%async_computation | async-start | bytes 4456448 | tf_op jit(solution)/shard_map/all_gather | solution.py:162
Sparse Core Ops, SparseCore 0:
  9.6 52.8 all-gather.4
  65.0 57.5 all-gather.2
